TPU v7x, 128 devices: a whole 4x4x4 slice. The times are simulated.
128 devices in a mesh: group: 8 (over z_lo, x), shard: 16 (over z_hi, y, core).
Axes of the slice: x: 4, y: 4, z: 4 (z_hi: 2, z_lo: 2; z = z_hi * 2 + z_lo), core: 2. Of those that a mesh axis runs over, the one named last changes fastest.
Arguments:
- src_emb: float32 [400, 262144], P(None, ('group', 'shard')), may hold values from -1.5 to 1.5
- src_state: float32 [262144], P(('group', 'shard')), may hold values from 0.1 to 1
- dst_emb: float32 [400, 8192], P(None, ('group', 'shard')), may hold values from -1.5 to 1.5
- dst_state: float32 [8192], P(('group', 'shard')), may hold values from 100 to 10000
- rel_table: float32 [400, 64], replicated, may hold values from -3 to 3
- rel_ids: int32 [2, 2, 8, 4], P(None, None, 'group'), may hold values from 0 to 63
- multiplicity: int32 [2, 2, 2048, 4], P(None, None, ('group', 'shard')), may hold values from 0 to 2
- neg_tile: int32 [2, 2, 2048], P(None, None, ('group', 'shard')), may hold values from 0 to 3
Outputs:
- src_out: float32 [400, 262144], P(None, ('group', 'shard'))
- src_state_out: float32 [262144], P(('group', 'shard'))
- dst_out: float32 [400, 8192], P(None, ('group', 'shard'))
- dst_state_out: float32 [8192], P(('group', 'shard'))
All inputs are finite; a program needn't handle non-finite values.
Results may differ from a plain program's by a relative error of at most 0.0004.
The roundings to bfloat16 on the way count: a program that leaves them out, or rounds other values in their place, can miss the bound.
Values may be sent and summed in bfloat16 or wider, within the bound.
No kernel may reach another device: no remote copies, remote signals or barrier semaphores. Data moves between devices by JAX's collectives and lax.ppermute only.
A program may use at most 64 MiB of HBM per device.

v0:
```python
import jax
import jax.numpy as jnp
from jax import lax
from jax.sharding import PartitionSpec as P

POOLS = 2
ROUNDS = 2
TILE = 128
LEARN_RATE = 0.1
POSITIVE_WEIGHT = 0.125
NEGATIVE_WEIGHT = 0.25
HIGHEST_PRECISION = lax.Precision.HIGHEST


def from_behind(value, axis, steps):
    count = lax.axis_size(axis)
    pairs = [(source, (source + steps) % count) for source in range(count)]
    return lax.ppermute(value, axis, pairs)


def column_tiles(offset, columns, tile_count):
    tile_of = (offset + lax.iota(jnp.int32, columns)) // TILE
    return (tile_of[None, :] == lax.iota(jnp.int32, tile_count)[:, None]).astype(jnp.float32)


def relation_columns(rel_table, rel_row, offset, columns):
    tile_count = rel_row.shape[0]
    chosen = (rel_row[None, :] == lax.iota(jnp.int32, rel_table.shape[1])[:, None]).astype(
        jnp.float32
    )
    per_tile = jnp.dot(rel_table, chosen, precision=HIGHEST_PRECISION)
    return jnp.dot(per_tile, column_tiles(offset, columns, tile_count), precision=HIGHEST_PRECISION)


def pair_gradient(scores, mult_f, neg_hot, offset, columns):
    col_tiles = column_tiles(offset, columns, mult_f.shape[1])
    positive = jnp.dot(mult_f, col_tiles, precision=HIGHEST_PRECISION)
    negative = jnp.dot(neg_hot, col_tiles, precision=HIGHEST_PRECISION)
    row_tiles = mult_f.shape[0]
    blocked = scores.reshape(row_tiles, TILE, columns)
    pair_grad = NEGATIVE_WEIGHT * negative[:, None, :] * jax.nn.sigmoid(
        blocked
    ) - POSITIVE_WEIGHT * positive[:, None, :] * jax.nn.sigmoid(-blocked)
    return pair_grad.reshape(row_tiles * TILE, columns).astype(jnp.bfloat16)


def adagrad(embedding, accum, gradient):
    new_accum = accum + jnp.mean(gradient * gradient, axis=0)
    return (embedding - LEARN_RATE * gradient / jnp.sqrt(new_accum)[None, :], new_accum)


def local(src_emb, src_state, dst_emb, dst_state, rel_table, rel_ids, multiplicity, neg_tile):
    pool_dev = dst_emb.shape[1] // POOLS
    shard_pos = lax.axis_index("shard")
    pool_cols = pool_dev * lax.axis_size("shard")
    tile_count = multiplicity.shape[3]
    for rotation in range(ROUNDS):
        if rotation > 0:
            dst_emb, dst_state = from_behind((dst_emb, dst_state), "group", 1)
        new_embs = []
        new_sums = []
        for pool_index in range(POOLS):
            local_pool = dst_emb[:, pool_index * pool_dev : (pool_index + 1) * pool_dev]
            local_sums = dst_state[pool_index * pool_dev : (pool_index + 1) * pool_dev]
            rel_row = rel_ids[rotation, pool_index, 0]
            mult_f = multiplicity[rotation, pool_index].astype(jnp.float32)
            neg_hot = (
                neg_tile[rotation, pool_index][:, None] == lax.iota(jnp.int32, tile_count)[None, :]
            ).astype(jnp.float32)
            own_scale = relation_columns(rel_table, rel_row, shard_pos * pool_dev, pool_dev)
            source_bf = src_emb.astype(jnp.bfloat16)
            gathered = lax.all_gather(local_pool, "shard", axis=1, tiled=True)
            scaled = (gathered * relation_columns(rel_table, rel_row, 0, pool_cols)).astype(
                jnp.bfloat16
            )
            scores = lax.dot_general(
                source_bf, scaled, (((0,), (0,)), ((), ())), preferred_element_type=jnp.float32
            )
            pair_grad = pair_gradient(scores, mult_f, neg_hot, 0, pool_cols)
            src_grad = lax.dot_general(
                scaled, pair_grad, (((1,), (1,)), ((), ())), preferred_element_type=jnp.float32
            )
            src_emb, src_state = adagrad(src_emb, src_state, src_grad)
            dest_part = jnp.dot(source_bf, pair_grad, preferred_element_type=jnp.float32)
            summed = lax.psum_scatter(dest_part, "shard", scatter_dimension=1, tiled=True)
            updated, updated_sums = adagrad(local_pool, local_sums, own_scale * summed)
            new_embs.append(updated)
            new_sums.append(updated_sums)
        dst_emb = jnp.concatenate(new_embs, axis=1)
        dst_state = jnp.concatenate(new_sums, axis=0)
    dst_emb, dst_state = from_behind((dst_emb, dst_state), "group", 1 - ROUNDS)
    return (src_emb, src_state, dst_emb, dst_state)


def solution(mesh):
    placed = (
        P(None, ("group", "shard")),
        P(("group", "shard")),
        P(None, ("group", "shard")),
        P(("group", "shard")),
        P(),
        P(None, None, "group", None),
        P(None, None, ("group", "shard"), None),
        P(None, None, ("group", "shard")),
    )
    return jax.shard_map(
        local,
        mesh=mesh,
        in_specs=placed,
        out_specs=(
            P(None, ("group", "shard")),
            P(("group", "shard")),
            P(None, ("group", "shard")),
            P(("group", "shard")),
        ),
        check_vma=False,
    )
```

profile of v0, /device:TPU:0, one launch (start us, length us, event | category | flops | bytes accessed | tf_op | source)
XLA Modules:
  0.0 458.4 jit_solution(17057751256044241185)
XLA Ops:
  8.1 0.9 fusion.12
  10.6 28.3 %all_gather.12 = f32[400,512]{0,1:T(8,128)S(1)} all-gather(f32[400,32]{0,1:T(8,128)S(1)} %get-tuple-element.27), channel_id=1, replica_groups=mesh['group'=8,'shard'=16] {'shard'}, dimensions={1}, use_global_device_ids=true | all-gather | bytes 870400 | tf_op jit(solution)/shard_map/all_gather | solution.py:72
  41.0 1.1 mul.212
  42.1 1.1 mul.217
  44.1 5.4 %fusion.1 = bf16[2048,512]{0,1:T(8,128)(2,1)S(1)} fusion(f32[64,8,16,128]{3,2,1,0:T(8,128)S(1)} %bitcast.133, f32[64,8,16,128]{3,2,1,0:T(8,128)S(1)} %bitcast.132, bf16[400,512]{1,0:T(8,128)(2,1)S(1)} %fusion.8, f32[400,2048]{1,0:T(8,128)S(1)} %copy-done.9), kind=kOutput, calls=%fused_computation.2 | convolution fusion | flops 849117184 | bytes 14172160 | tf_op jit(solution)/shard_map/dot_general | solution.py:76
  49.5 1.0 multiply_reduce_fusion.3
  51.0 23.7 %all_gather.13 = f32[400,512]{0,1:T(8,128)} all-gather(f32[400,32]{0,1:T(8,128)S(1)} %get-tuple-element.26), channel_id=1, replica_groups=mesh['group'=8,'shard'=16] {'shard'}, dimensions={1}, use_global_device_ids=true | all-gather | bytes 870400 | tf_op jit(solution)/shard_map/all_gather | solution.py:72
  74.8 2.4 copy.27
  77.4 2.7 divide_subtract_fusion.3
  80.7 3.2 fusion.7
  83.9 2.3 convolution_bitcast_fusion.2
  86.5 3.6 convolution_bitcast_fusion.3
  90.1 1.3 copy.40
  91.5 2.7 multiply_reduce_fusion.2
  96.1 1.5 fusion.37
  99.8 1.5 fusion.36
  101.2 3.7 divide_subtract_fusion.2
  105.0 46.3 %reduce-scatter.15.cloned.1.call-done = f32[32,400]{1,0:T(8,128)} async-done(((f32[512,400]{1,0:T(8,128)}), f32[32,400]{1,0:T(8,128)}) %reduce-scatter.15.cloned.1.call-update) | async-done | bytes 51216
  151.3 2.3 multiply_reduce_fusion.6
  153.6 67.5 %reduce-scatter.13.cloned.1.call-done = f32[32,400]{1,0:T(8,128)} async-done(((f32[512,400]{1,0:T(8,128)}), f32[32,400]{1,0:T(8,128)}) %reduce-scatter.13.cloned.1.call-update) | async-done | bytes 51216
  221.1 1.2 multiply_reduce_fusion.7
  222.3 1.3 fusion.78
  223.6 0.9 divide_subtract_fusion.7
  224.6 1.6 collective-permute-start
  226.1 1.5 convolution_multiply_fusion.7
  227.6 4.1 collective-permute-done
  232.3 25.8 %all_gather.14 = f32[400,512]{0,1:T(8,128)} all-gather(f32[400,32]{0,1:T(8,128)S(1)} %get-tuple-element.23), channel_id=1, replica_groups=mesh['group'=8,'shard'=16] {'shard'}, dimensions={1}, use_global_device_ids=true | all-gather | bytes 870400 | tf_op jit(solution)/shard_map/all_gather | solution.py:72
  258.2 2.4 copy.31
  260.6 1.5 multiply_convert_fusion.1
  262.1 4.0 fusion.5
  266.1 3.3 multiply_reduce_fusion.1
  269.4 22.3 %all_gather.15 = f32[400,512]{0,1:T(8,128)S(1)} all-gather(f32[400,32]{0,1:T(8,128)S(1)} %copy-done.12), channel_id=1, replica_groups=mesh['group'=8,'shard'=16] {'shard'}, dimensions={1}, use_global_device_ids=true | all-gather | bytes 870400 | tf_op jit(solution)/shard_map/all_gather | solution.py:72
  291.7 1.2 copy.32
  293.7 3.7 divide_subtract_fusion.1
  298.4 3.2 fusion.3
  301.6 1.3 copy-done.4
  303.0 2.3 convolution_bitcast_fusion
  305.6 4.9 %convolution_bitcast_fusion.1 = f32[512,400]{1,0:T(8,128)} fusion(bf16[2048,512]{1,0:T(8,128)(2,1)} %copy-done.3, f32[400,2048]{1,0:T(8,128)} %copy-done.1), kind=kOutput, calls=%fused_computation.25 | convolution fusion | flops 839680000 | bytes 6193152
  310.5 1.2 pad_maximum_fusion.2
  311.7 4.5 multiply_reduce_fusion
  316.8 53.0 %reduce-scatter.19.cloned.1.call-done = f32[32,400]{1,0:T(8,128)} async-done(((f32[512,400]{1,0:T(8,128)}), f32[32,400]{1,0:T(8,128)}) %reduce-scatter.19.cloned.1.call-update) | async-done | bytes 51216
  369.9 2.3 multiply_reduce_fusion.4
  372.2 67.4 %reduce-scatter.17.cloned.1.call-done = f32[32,400]{1,0:T(8,128)} async-done(((f32[512,400]{1,0:T(8,128)}), f32[32,400]{1,0:T(8,128)}) %reduce-scatter.17.cloned.1.call-update) | async-done | bytes 51216
  439.5 1.2 multiply_reduce_fusion.5
  441.6 2.9 collective-permute-start.3
  444.5 0.9 divide_subtract_fusion.5
  445.4 0.9 collective-permute-start.2
  446.4 4.3 divide_subtract_fusion
  (91 shorter events, 16.2 us)
Async XLA Ops:
  7.2 33.0 %copy-start = (f32[400,64]{0,1:T(8,128)S(1)}, f32[400,64]{0,1:T(8,128)}, u32[]{:S(2)}) copy-start(f32[400,64]{0,1:T(8,128)} %param.12) | copy-start | bytes 307204
  7.2 32.0 %copy-start.21 = (s32[2,2,16]{2,1,0:T(2,128)S(1)}, s32[2,2,16]{2,1,0:T(2,128)}, u32[]{:S(2)}) copy-start(s32[2,2,16]{2,1,0:T(2,128)} %param.15) | copy-start | bytes 772
  7.2 144.1 %reduce-scatter.15.cloned.1.call-start = ((), (), s32[]{:S(2)}) async-start(), calls=%async_computation.5 | async-start | bytes 1114112
  7.2 92.5 %copy-start.17 = (s32[512]{0:T(512)}, s32[512]{0:T(512)S(1)}, u32[]{:S(2)}) copy-start(s32[512]{0:T(512)S(1)} %add_select_fusion) | copy-start | bytes 6148
  40.4 2.9 copy-start.13
  42.1 1.9 copy-start.9
  49.5 1.3 copy-start.10
  49.5 27.7 %copy-start.22 = (s32[16]{0:T(128)S(1)}, s32[16]{0:T(128)}, u32[]{:S(2)}) copy-start(s32[16]{0:T(128)} %get-tuple-element.29) | copy-start | bytes 196
  49.5 27.8 %copy-start.20 = (f32[2048]{0:T(1024)S(1)}, f32[2048]{0:T(1024)}, u32[]{:S(2)}) copy-start(f32[2048]{0:T(1024)} %param.9) | copy-start | bytes 24580
  51.0 29.1 %copy-start.14 = (f32[4,400]{1,0:T(4,128)}, f32[4,400]{1,0:T(4,128)S(1)}, u32[]{:S(2)}) copy-start(f32[4,400]{1,0:T(4,128)S(1)} %fusion.29) | copy-start | bytes 19204
  77.4 2.7 copy-start.6
  80.1 3.8 copy-start.2
  86.3 134.8 %reduce-scatter.13.cloned.1.call-start = ((), (), s32[]{:S(2)}) async-start(), calls=%async_computation.4 | async-start | bytes 1114112
  91.5 278.4 %reduce-scatter.19.cloned.1.call-start = ((), (), s32[]{:S(2)}) async-start(), calls=%async_computation.7 | async-start | bytes 1114112
  91.5 2.7 copy-start.23
  101.2 122.4 %copy-start.11 = (f32[400,64]{0,1:T(8,128)S(1)}, f32[400,64]{0,1:T(8,128)}, u32[]{:S(2)}) copy-start(f32[400,64]{0,1:T(8,128)} %param.10) | copy-start | bytes 307204
  105.0 161.1 %copy-start.1 = (f32[400,2048]{1,0:T(8,128)}, f32[400,2048]{1,0:T(8,128)S(1)}, u32[]{:S(2)}) copy-start(f32[400,2048]{1,0:T(8,128)S(1)} %divide_subtract_fusion.2) | copy-start | bytes 9830404
  224.6 7.1 %collective-permute-start = (f32[400,64]{0,1:T(8,128)S(1)}, f32[400,64]{0,1:T(8,128)S(1)}, u32[]{:S(2)}, u32[]{:S(2)}) collective-permute-start(f32[400,64]{0,1:T(8,128)S(1)} %pad_maximum_fusion), channel_id=1, source_target_pairs={{0,16},{16,32},{32,48},{48,64},{64,80},{80,96},{96,112},{112,0},{1... | collective-permute-start | bytes 307208 | tf_op jit(solution)/shard_map/ppermute | solution.py:18
  266.1 3.3 copy-start.3
  266.1 3.3 copy-start.12
  293.7 3.8 copy-start.7
  293.7 3.8 copy-start.8
  293.7 4.7 %copy-start.18 = (f32[16,512]{1,0:T(8,128)S(1)}, f32[16,512]{1,0:T(8,128)}, u32[]{:S(2)}) copy-start(f32[16,512]{1,0:T(8,128)} %fusion.10) | copy-start | bytes 98308
  293.7 4.7 %copy-start.19 = (f32[16,512]{1,0:T(8,128)S(1)}, f32[16,512]{1,0:T(8,128)}, u32[]{:S(2)}) copy-start(f32[16,512]{1,0:T(8,128)} %convolution_multiply_fusion.7) | copy-start | bytes 98308
  297.7 0.8 copy-start.5
  301.6 1.3 copy-start.4
  305.3 134.3 %reduce-scatter.17.cloned.1.call-start = ((), (), s32[]{:S(2)}) async-start(), calls=%async_computation.6 | async-start | bytes 1114112
  311.7 4.6 copy-start.15
  311.7 4.6 copy-start.16
  311.7 129.0 %collective-permute-start.1 = (f32[64]{0:T(128)}, f32[64]{0:T(128)}, u32[]{:S(2)}, u32[]{:S(2)}) collective-permute-start(f32[64]{0:T(128)} %pad_maximum_fusion.2), channel_id=1, source_target_pairs={{0,16},{16,32},{32,48},{48,64},{64,80},{80,96},{96,112},{112,0},{1... | collective-permute-start | bytes 776 | tf_op jit(solution)/shard_map/ppermute | solution.py:18
  441.6 9.1 %collective-permute-start.3 = (f32[64]{0:T(128)S(1)}, f32[64]{0:T(128)S(1)}, u32[]{:S(2)}, u32[]{:S(2)}) collective-permute-start(f32[64]{0:T(128)S(1)} %pad_maximum_fusion.3), channel_id=1, source_target_pairs={{0,112},{16,0},{32,16},{48,32},{64,48},{80,64},{96,80},{112,96},{1... | collective-permute-start | bytes 776 | tf_op jit(solution)/shard_map/ppermute | solution.py:18
  445.4 5.2 %collective-permute-start.2 = (f32[400,64]{0,1:T(8,128)S(1)}, f32[400,64]{0,1:T(8,128)S(1)}, u32[]{:S(2)}, u32[]{:S(2)}) collective-permute-start(f32[400,64]{0,1:T(8,128)S(1)} %pad_maximum_fusion.1), channel_id=1, source_target_pairs={{0,112},{16,0},{32,16},{48,32},{64,48},{80,64},{96,80},{112,96},{1... | collective-permute-start | bytes 307208 | tf_op jit(solution)/shard_map/ppermute | solution.py:18
Sparse Core Ops, SparseCore 0:
  86.4 64.8 reduce-scatter.14
  155.1 65.9 reduce-scatter.12
  305.4 64.4 reduce-scatter.18
  373.6 65.9 reduce-scatter.16
where the time goes:
time: 459 us; the launch traced here: 458 us
  waiting for transfers between devices  238 us (52%)
  blocking collectives  100 us (22%)
  matrix products  58.5 us (13%)
  other arithmetic  24 us (5%)
  local copies, waits for them, and re-layouts  17.4 us (4%)
  between operations  14.2 us (3%)
  starting transfers between devices  5.95 us (1%)
    unnamed x8, waiting for transfers between devices  234 us
    all_gather x4, blocking collectives, local(): gathered = lax.all_gather(local_pool, 'shard', axis=1, tiled=True)  100 us
    sub x6, other arithmetic, adagrad(): embedding - LEARN_RATE * gradient / jnp.sqrt(new_accum)[None, :]  16.3 us
    dot_general x4, matrix products, local(): lax.dot_general(source_bf, scaled, (((0,), (0,)), ((), ())), preferred_el...  15.8 us
    dot_general x4, matrix products, local(): lax.dot_general(scaled, pair_grad, (((1,), (1,)), ((), ())), preferred_el...  11.6 us
    dot_general x8, matrix products, relation_columns(): jnp.dot(per_tile, column_tiles(offset, columns, tile_count), precision=HI...  11.1 us
    unnamed x3, matrix products  9.51 us
  transfers between devices with their start and end apart: 8, of which 5 were waited for; matrix products, arithmetic and copies ran while one was open for 9% of the time, Pallas kernels for 0%

commit v1 on v0

--- a/solution.py
+++ b/solution.py
@@ -69,7 +69,10 @@
             ).astype(jnp.float32)
             own_scale = relation_columns(rel_table, rel_row, shard_pos * pool_dev, pool_dev)
             source_bf = src_emb.astype(jnp.bfloat16)
-            gathered = lax.all_gather(local_pool, "shard", axis=1, tiled=True)
+            gathered = jnp.concatenate(
+                lax.all_to_all(jnp.stack([local_pool] * lax.axis_size("shard")), "shard", 0, 0),
+                axis=1,
+            )
             scaled = (gathered * relation_columns(rel_table, rel_row, 0, pool_cols)).astype(
                 jnp.bfloat16
             )

time: 459 us -> 409 us (0.89)
  blocking collectives: 100 us -> 0 us
  waiting for transfers between devices: 238 us -> 263 us
  starting transfers between devices: 5.95 us -> 27.5 us
    unnamed x8 -> x4, waiting for transfers between devices: 234 us -> 0.07 us
    reduce_scatter x0 -> x4, waiting for transfers between devices: none -> 230 us  [local(): lax.psum_scatter(dest_part, 'shard', scatter_dimension=1, tiled=True)]
    all_gather x4 -> x0, blocking collectives: 100 us -> none  [local(): gathered = lax.all_gather(local_pool, 'shard', axis=1, tiled=True)]
    all_to_all x0 -> x4, waiting for transfers between devices: none -> 32.5 us  [local(): lax.all_to_all(jnp.stack([local_pool] * lax.axis_size('shard')), 'shard',...]
    all_to_all x0 -> x4, starting transfers between devices: none -> 20.7 us  [local(): lax.all_to_all(jnp.stack([local_pool] * lax.axis_size('shard')), 'shard',...]
    unnamed x3 -> x0, matrix products: 9.51 us -> none
    all_gather x4 -> x0, local copies, waits for them, and re-layouts: 6.39 us -> none  [local(): gathered = lax.all_gather(local_pool, 'shard', axis=1, tiled=True)]
    dot_general x1 -> x4, matrix products: 3.61 us -> 9.17 us  [local(): jnp.dot(source_bf, pair_grad, preferred_element_type=jnp.float32)]
  transfers between devices with their start and end apart: 8 -> 12, of which waited for: 5 -> 9; matrix products, arithmetic and copies ran while one was open for 9% -> 21% of each run, Pallas kernels for 0% -> 0%
where the time goes in v1:
time: 409 us; the launch traced here: 408 us
  waiting for transfers between devices  263 us (64%)
  matrix products  58.6 us (14%)
  starting transfers between devices  27.5 us (7%)
  other arithmetic  24.1 us (6%)
  local copies, waits for them, and re-layouts  20.8 us (5%)
  between operations  14.2 us (3%)
    reduce_scatter x4, waiting for transfers between devices, local(): lax.psum_scatter(dest_part, 'shard', scatter_dimension=1, tiled=True)  230 us
    all_to_all x4, waiting for transfers between devices, local(): lax.all_to_all(jnp.stack([local_pool] * lax.axis_size('shard')), 'shard',...  32.5 us
    all_to_all x4, starting transfers between devices, local(): lax.all_to_all(jnp.stack([local_pool] * lax.axis_size('shard')), 'shard',...  20.7 us
    sub x6, other arithmetic, adagrad(): embedding - LEARN_RATE * gradient / jnp.sqrt(new_accum)[None, :]  18 us
    dot_general x4, matrix products, local(): lax.dot_general(source_bf, scaled, (((0,), (0,)), ((), ())), preferred_el...  15.9 us
    dot_general x4, matrix products, local(): lax.dot_general(scaled, pair_grad, (((1,), (1,)), ((), ())), preferred_el...  15.7 us
    dot_general x8, matrix products, relation_columns(): jnp.dot(per_tile, column_tiles(offset, columns, tile_count), precision=HI...  11.1 us
    dot_general x4, matrix products, local(): jnp.dot(source_bf, pair_grad, preferred_element_type=jnp.float32)  9.17 us
  transfers between devices with their start and end apart: 12, of which 9 were waited for; matrix products, arithmetic and copies ran while one was open for 21% of the time, Pallas kernels for 0%

profile of v1, /device:TPU:0, one launch (start us, length us, event | category | flops | bytes accessed | tf_op | source)
XLA Modules:
  0.0 408.1 jit_solution(5938208853850203609)
XLA Ops:
  9.2 8.0 %all-to-all-start = ((f32[16,400,32]{1,2,0:T(8,128)}), f32[16,400,32]{1,2,0:T(8,128)S(1)}, u32[]{:S(2)}, u32[]{:S(2)}) async-start(f32[16,400,32]{1,2,0:T(8,128)} %stack.8), calls=%async_computation | async-start | bytes 2097152 | tf_op jit(solution)/shard_map/all_to_all | solution.py:73
  21.6 13.6 %all-to-all-done = f32[16,400,32]{1,2,0:T(8,128)S(1)} async-done(((f32[16,400,32]{1,2,0:T(8,128)}), f32[16,400,32]{1,2,0:T(8,128)S(1)}, u32[]{:S(2)}, u32[]{:S(2)}) %all-to-all-start) | async-done | bytes 819232 | tf_op jit(solution)/shard_map/all_to_all | solution.py:73
  35.2 1.1 stack.9
  36.3 3.7 all-to-all-start.1
  40.9 2.1 mul.212
  45.0 5.4 %fusion.1 = bf16[2048,512]{0,1:T(8,128)(2,1)S(1)} fusion(f32[64,8,16,128]{3,2,1,0:T(8,128)S(1)} %bitcast.131, f32[64,8,16,128]{3,2,1,0:T(8,128)S(1)} %bitcast.130, bf16[400,512]{1,0:T(8,128)(2,1)S(1)} %fusion.8, f32[400,2048]{1,0:T(8,128)S(1)} %copy-done.6), kind=kOutput, calls=%fused_computation.2 | convolution fusion | flops 849117184 | bytes 14172160 | tf_op jit(solution)/shard_map/dot_general | solution.py:79
  50.4 2.7 multiply_reduce_fusion.3
  53.1 2.3 convolution_bitcast_fusion
  55.4 2.5 all-to-all-done.1
  59.1 3.7 divide_subtract_fusion.3
  62.8 3.2 fusion.7
  66.1 1.3 copy-done.2
  67.4 2.3 fusion.22
  70.3 1.5 fusion.10
  71.8 1.5 fusion.11
  74.3 50.3 %reduce-scatter.5.cloned.1.call-done = f32[400,32]{0,1:T(8,128)} async-done(((f32[400,512]{0,1:T(8,128)}), f32[400,32]{0,1:T(8,128)}) %reduce-scatter.5.cloned.1.call-update) | async-done | bytes 51216 | tf_op jit(solution)/shard_map/reduce_scatter | solution.py:88
  124.6 2.3 multiply_reduce_fusion.7
  127.0 68.1 %reduce-scatter.7.cloned.1.call-done = f32[400,32]{0,1:T(8,128)} async-done(((f32[400,512]{0,1:T(8,128)}), f32[400,32]{0,1:T(8,128)}) %reduce-scatter.7.cloned.1.call-update) | async-done | bytes 51216 | tf_op jit(solution)/shard_map/reduce_scatter | solution.py:88
  195.0 1.2 multiply_reduce_fusion.6
  196.2 1.4 fusion.81
  198.5 1.5 collective-permute-start
  200.1 5.1 %multiply_reduce_fusion.2 = (f32[2048]{0:T(1024)}, f32[400,2048]{1,0:T(8,128)}) fusion(bf16[400,512]{1,0:T(8,128)(2,1)} %copy-done.4, bf16[2048,512]{1,0:T(8,128)(2,1)} %copy-done.2), kind=kOutput, calls=%fused_computation.21 | convolution fusion | flops 840497152 | bytes 5791744 | tf_op jit(solution)/shard_map/dot_general | solution.py:83
  207.4 4.7 %all-to-all-start.2 = ((f32[16,400,32]{1,2,0:T(8,128)}), f32[16,400,32]{1,2,0:T(8,128)}, u32[]{:S(2)}, u32[]{:S(2)}) async-start(f32[16,400,32]{1,2,0:T(8,128)} %stack.10), calls=%async_computation.4 | async-start | bytes 2097152 | tf_op jit(solution)/shard_map/all_to_all | solution.py:73
  212.1 1.3 fusion.83
  213.5 4.4 %divide_subtract_fusion.2 = f32[400,2048]{1,0:T(8,128)} fusion(f32[400,2048]{1,0:T(8,128)S(1)} %divide_subtract_fusion.3, f32[400,2048]{1,0:T(8,128)} %get-tuple-element.39, f32[2048]{0:T(1024)S(1)} %get-tuple-element.14), kind=kLoop, calls=%fused_computation.20 | loop fusion | flops 2457600 | bytes 9838592 | tf_op jit(solution)/shard_map/sub | solution.py:49
  217.8 12.3 %all-to-all-done.2 = f32[16,400,32]{1,2,0:T(8,128)} async-done(((f32[16,400,32]{1,2,0:T(8,128)}), f32[16,400,32]{1,2,0:T(8,128)}, u32[]{:S(2)}, u32[]{:S(2)}) %all-to-all-start.2) | async-done | bytes 819232 | tf_op jit(solution)/shard_map/all_to_all | solution.py:73
  230.1 2.0 stack.11
  232.1 4.4 %all-to-all-start.3 = ((f32[16,400,32]{1,2,0:T(8,128)}), f32[16,400,32]{1,2,0:T(8,128)}, u32[]{:S(2)}, u32[]{:S(2)}) async-start(f32[16,400,32]{1,2,0:T(8,128)} %stack.11), calls=%async_computation.5 | async-start | bytes 2097152 | tf_op jit(solution)/shard_map/all_to_all | solution.py:73
  236.5 2.4 copy.24
  238.9 1.7 multiply_convert_fusion.1
  240.6 4.0 fusion.5
  244.6 3.4 multiply_reduce_fusion.1
  248.0 2.3 fusion.18
  250.3 4.1 %all-to-all-done.3 = f32[16,400,32]{1,2,0:T(8,128)} async-done(((f32[16,400,32]{1,2,0:T(8,128)}), f32[16,400,32]{1,2,0:T(8,128)}, u32[]{:S(2)}, u32[]{:S(2)}) %all-to-all-start.3) | async-done | bytes 819232 | tf_op jit(solution)/shard_map/all_to_all | solution.py:73
  254.4 1.5 copy.25
  256.2 1.2 multiply_convert_fusion
  257.5 3.7 divide_subtract_fusion.1
  261.3 3.2 fusion.3
  264.6 1.3 copy-done.3
  265.9 2.3 fusion.14
  268.2 1.3 pad_maximum_fusion.2
  270.5 4.5 %multiply_reduce_fusion = (f32[2048]{0:T(1024)S(1)}, f32[400,2048]{1,0:T(8,128)}) fusion(bf16[400,512]{1,0:T(8,128)(2,1)} %copy-done.5, bf16[2048,512]{1,0:T(8,128)(2,1)} %copy-done.3), kind=kOutput, calls=%fused_computation.17 | convolution fusion | flops 840497152 | bytes 5791744 | tf_op jit(solution)/shard_map/dot_general | solution.py:83
  275.6 44.0 %reduce-scatter.9.cloned.1.call-done = f32[400,32]{0,1:T(8,128)} async-done(((f32[400,512]{0,1:T(8,128)}), f32[400,32]{0,1:T(8,128)}) %reduce-scatter.9.cloned.1.call-update) | async-done | bytes 51216 | tf_op jit(solution)/shard_map/reduce_scatter | solution.py:88
  319.6 2.3 multiply_reduce_fusion.5
  321.9 67.4 %reduce-scatter.11.cloned.1.call-done = f32[400,32]{0,1:T(8,128)} async-done(((f32[400,512]{0,1:T(8,128)}), f32[400,32]{0,1:T(8,128)}) %reduce-scatter.11.cloned.1.call-update) | async-done | bytes 51216 | tf_op jit(solution)/shard_map/reduce_scatter | solution.py:88
  389.3 1.2 multiply_reduce_fusion.4
  391.3 2.9 collective-permute-start.3
  396.1 4.3 %divide_subtract_fusion = f32[400,2048]{1,0:T(8,128)} fusion(f32[400,2048]{1,0:T(8,128)S(1)} %divide_subtract_fusion.1, f32[400,2048]{1,0:T(8,128)} %get-tuple-element.47, f32[2048]{0:T(1024)} %get-tuple-element.8), kind=kLoop, calls=%fused_computation.16 | loop fusion | flops 2457600 | bytes 9838592 | tf_op jit(solution)/shard_map/sub | solution.py:49
  (92 shorter events, 20.9 us)
Async XLA Ops:
  7.2 14.0 %copy-start = (f32[400,64]{0,1:T(8,128)S(1)}, f32[400,64]{0,1:T(8,128)}, u32[]{:S(2)}) copy-start(f32[400,64]{0,1:T(8,128)} %param.12) | copy-start | bytes 307204
  7.2 10.1 %copy-start.19 = (s32[2,2,16]{2,1,0:T(2,128)S(1)}, s32[2,2,16]{2,1,0:T(2,128)}, u32[]{:S(2)}) copy-start(s32[2,2,16]{2,1,0:T(2,128)} %param.15) | copy-start | bytes 772
  7.2 12.1 %copy-start.21 = (s32[2,2,16,4]{2,3,1,0:T(4,128)S(1)}, s32[2,2,16,4]{2,3,1,0:T(4,128)}, u32[]{:S(2)}) copy-start(s32[2,2,16,4]{2,3,1,0:T(4,128)} %param.14) | copy-start | bytes 3076
  7.2 12.3 %copy-start.20 = (s32[2,2,1,4]{3,2,1,0:T(1,128)S(1)}, s32[2,2,1,4]{3,2,1,0:T(1,128)}, u32[]{:S(2)}) copy-start(s32[2,2,1,4]{3,2,1,0:T(1,128)} %param.13) | copy-start | bytes 196
  9.2 26.0 %all-to-all-start = ((f32[16,400,32]{1,2,0:T(8,128)}), f32[16,400,32]{1,2,0:T(8,128)S(1)}, u32[]{:S(2)}, u32[]{:S(2)}) async-start(f32[16,400,32]{1,2,0:T(8,128)} %stack.8), calls=%async_computation | async-start | bytes 2097152 | tf_op jit(solution)/shard_map/all_to_all | solution.py:73
  17.3 54.5 %copy-start.15 = (s32[512]{0:T(512)}, s32[512]{0:T(512)S(1)}, u32[]{:S(2)}) copy-start(s32[512]{0:T(512)S(1)} %add_select_fusion) | copy-start | bytes 6148
  21.4 37.1 %copy-start.9 = (f32[4,400]{1,0:T(4,128)}, f32[4,400]{1,0:T(4,128)S(1)}, u32[]{:S(2)}) copy-start(f32[4,400]{1,0:T(4,128)S(1)} %fusion.32) | copy-start | bytes 19204
  21.6 21.4 %copy-start.10 = (f32[4,400]{1,0:T(4,128)}, f32[4,400]{1,0:T(4,128)S(1)}, u32[]{:S(2)}) copy-start(f32[4,400]{1,0:T(4,128)S(1)} %fusion.31) | copy-start | bytes 19204
  36.3 21.6 %all-to-all-start.1 = ((f32[16,400,32]{1,2,0:T(8,128)}), f32[16,400,32]{1,2,0:T(8,128)S(1)}, u32[]{:S(2)}, u32[]{:S(2)}) async-start(f32[16,400,32]{1,2,0:T(8,128)} %stack.9), calls=%async_computation.1 | async-start | bytes 2097152 | tf_op jit(solution)/shard_map/all_to_all | solution.py:73
  40.0 84.6 %reduce-scatter.5.cloned.1.call-start = ((), (), s32[]{:S(2)}) async-start(), calls=%async_computation.8 | async-start | bytes 1114112 | tf_op jit(solution)/shard_map/reduce_scatter | solution.py:88
  43.0 1.9 copy-start.6
  53.1 5.9 %copy-start.8 = (f32[2048]{0:T(1024)}, f32[2048]{0:T(1024)S(1)}, u32[]{:S(2)}) copy-start(f32[2048]{0:T(1024)S(1)} %get-tuple-element.36) | copy-start | bytes 24580
  55.4 3.7 copy-start.18
  58.3 136.8 %reduce-scatter.7.cloned.1.call-start = ((), (), s32[]{:S(2)}) async-start(), calls=%async_computation.9 | async-start | bytes 1114112 | tf_op jit(solution)/shard_map/reduce_scatter | solution.py:88
  59.1 3.8 copy-start.4
  66.1 1.3 copy-start.2
  67.4 130.2 %copy-start.7 = (f32[400,64]{0,1:T(8,128)S(1)}, f32[400,64]{0,1:T(8,128)}, u32[]{:S(2)}) copy-start(f32[400,64]{0,1:T(8,128)} %param.10) | copy-start | bytes 307204
  198.5 7.1 %collective-permute-start = (f32[400,64]{0,1:T(8,128)S(1)}, f32[400,64]{0,1:T(8,128)S(1)}, u32[]{:S(2)}, u32[]{:S(2)}) collective-permute-start(f32[400,64]{0,1:T(8,128)S(1)} %pad_maximum_fusion), channel_id=1, source_target_pairs={{0,16},{16,32},{32,48},{48,64},{64,80},{80,96},{96,112},{112,0},{1... | collective-permute-start | bytes 307208 | tf_op jit(solution)/shard_map/ppermute | solution.py:18
  207.4 22.7 %all-to-all-start.2 = ((f32[16,400,32]{1,2,0:T(8,128)}), f32[16,400,32]{1,2,0:T(8,128)}, u32[]{:S(2)}, u32[]{:S(2)}) async-start(f32[16,400,32]{1,2,0:T(8,128)} %stack.10), calls=%async_computation.4 | async-start | bytes 2097152 | tf_op jit(solution)/shard_map/all_to_all | solution.py:73
  217.8 22.8 %copy-start.1 = (f32[400,2048]{1,0:T(8,128)S(1)}, f32[400,2048]{1,0:T(8,128)}, u32[]{:S(2)}) copy-start(f32[400,2048]{1,0:T(8,128)} %divide_subtract_fusion.2) | copy-start | bytes 9830404
  232.1 22.3 %all-to-all-start.3 = ((f32[16,400,32]{1,2,0:T(8,128)}), f32[16,400,32]{1,2,0:T(8,128)}, u32[]{:S(2)}, u32[]{:S(2)}) async-start(f32[16,400,32]{1,2,0:T(8,128)} %stack.11), calls=%async_computation.5 | async-start | bytes 2097152 | tf_op jit(solution)/shard_map/all_to_all | solution.py:73
  236.5 83.2 %reduce-scatter.9.cloned.1.call-start = ((), (), s32[]{:S(2)}) async-start(), calls=%async_computation.10 | async-start | bytes 1114112 | tf_op jit(solution)/shard_map/reduce_scatter | solution.py:88
  250.3 7.2 %copy-start.11 = (f32[2048]{0:T(1024)S(1)}, f32[2048]{0:T(1024)}, u32[]{:S(2)}) copy-start(f32[2048]{0:T(1024)} %get-tuple-element.15) | copy-start | bytes 24580
  250.3 7.2 %copy-start.13 = (f32[2048]{0:T(1024)S(1)}, f32[2048]{0:T(1024)}, u32[]{:S(2)}) copy-start(f32[2048]{0:T(1024)} %get-tuple-element.44) | copy-start | bytes 24580
  256.0 133.3 %reduce-scatter.11.cloned.1.call-start = ((), (), s32[]{:S(2)}) async-start(), calls=%async_computation.11 | async-start | bytes 1114112 | tf_op jit(solution)/shard_map/reduce_scatter | solution.py:88
  257.5 3.8 copy-start.5
  257.5 3.8 copy-start.16
  257.5 3.8 copy-start.17
  264.5 1.3 copy-start.3
  269.6 5.5 %copy-start.12 = (f32[2048]{0:T(1024)S(1)}, f32[2048]{0:T(1024)}, u32[]{:S(2)}) copy-start(f32[2048]{0:T(1024)} %get-tuple-element.15) | copy-start | bytes 24580
  269.6 5.5 %copy-start.14 = (f32[2048]{0:T(1024)S(1)}, f32[2048]{0:T(1024)}, u32[]{:S(2)}) copy-start(f32[2048]{0:T(1024)} %get-tuple-element.44) | copy-start | bytes 24580
  269.6 120.9 %collective-permute-start.1 = (f32[64]{0:T(128)}, f32[64]{0:T(128)}, u32[]{:S(2)}, u32[]{:S(2)}) collective-permute-start(f32[64]{0:T(128)} %pad_maximum_fusion.2), channel_id=1, source_target_pairs={{0,16},{16,32},{32,48},{48,64},{64,80},{80,96},{96,112},{112,0},{1... | collective-permute-start | bytes 776 | tf_op jit(solution)/shard_map/ppermute | solution.py:18
  391.3 9.1 %collective-permute-start.3 = (f32[64]{0:T(128)S(1)}, f32[64]{0:T(128)S(1)}, u32[]{:S(2)}, u32[]{:S(2)}) collective-permute-start(f32[64]{0:T(128)S(1)} %pad_maximum_fusion.3), channel_id=1, source_target_pairs={{0,112},{16,0},{32,16},{48,32},{64,48},{80,64},{96,80},{112,96},{1... | collective-permute-start | bytes 776 | tf_op jit(solution)/shard_map/ppermute | solution.py:18
  395.2 5.3 %collective-permute-start.2 = (f32[400,64]{0,1:T(8,128)S(1)}, f32[400,64]{0,1:T(8,128)S(1)}, u32[]{:S(2)}, u32[]{:S(2)}) collective-permute-start(f32[400,64]{0,1:T(8,128)S(1)} %pad_maximum_fusion.1), channel_id=1, source_target_pairs={{0,112},{16,0},{32,16},{48,32},{64,48},{80,64},{96,80},{112,96},{1... | collective-permute-start | bytes 307208 | tf_op jit(solution)/shard_map/ppermute | solution.py:18
Sparse Core Ops, SparseCore 0:
  58.4 66.2 reduce-scatter.4
  129.0 65.9 reduce-scatter.6
  256.1 63.4 reduce-scatter.8
  323.3 65.9 reduce-scatter.10
